TPU v7x, 256 devices: a whole 4x4x8 slice. The times are simulated.
256 devices in a mesh: group: 2 (over core), ctx: 32 (over x, z_hi, y), tp: 4 (over z_lo).
Axes of the slice: x: 4, y: 4, z: 8 (z_hi: 2, z_lo: 4; z = z_hi * 4 + z_lo), core: 2. Of those that a mesh axis runs over, the one named last changes fastest.
Arguments:
- activations: bfloat16 [8192, 8192], P(('group', 'ctx')), may hold values from -6 to 6
- queries: bfloat16 [8192, 4096], P(('group', 'ctx'), 'tp'), may hold values from -400 to 400
- out_grad: bfloat16 [8192, 4096], P(('group', 'ctx'), 'tp'), may hold values from -6 to 6
- key_weight: bfloat16 [8192, 512], P('ctx', 'tp'), may hold values from -0.0625 to 0.0625
- value_weight: bfloat16 [8192, 512], P('ctx', 'tp'), may hold values from -0.0625 to 0.0625
- sessions: int32 [32, 128], P('ctx'), may hold values from 0 to 3, never falling along the last dimension, each value on 1 to 64 neighbouring positions
Outputs:
- attention: bfloat16 [8192, 4096], P(('group', 'ctx'), 'tp')
- query_grad: bfloat16 [8192, 4096], P(('group', 'ctx'), 'tp')
- key_weight_grad: float32 [8192, 512], P(('group', 'ctx'), 'tp')
- value_weight_grad: float32 [8192, 512], P(('group', 'ctx'), 'tp')
- input_grad: bfloat16 [8192, 8192], P(('group', 'ctx'), 'tp')
Inputs may be any that keep to these rules, and one draw needn't show every extreme that they name: `sessions`: each row never falls; every session in a row has 1 to 64 tokens, and one session of each row has exactly that many.
All inputs are finite; a program needn't handle non-finite values.
Results may differ from a plain program's by a relative error of at most 0.025.
The roundings to bfloat16 on the way count: a program that leaves them out, or rounds other values in their place, can miss the bound.
Values may be sent and summed in bfloat16 or wider, within the bound.
No kernel may reach another device: no remote copies, remote signals or barrier semaphores. Data moves between devices by JAX's collectives and lax.ppermute only.
A program may use at most 64 MiB of HBM per device.

v0:
```python
import math
import jax
import jax.numpy as jnp
from jax import lax
from jax.sharding import PartitionSpec as P

HQ = 32
KVH = 4
HD = 128
THETA = 500000.0


def cut_along(array, dim, count):
    before, after = (array.shape[:dim], array.shape[dim + 1 :])
    return jnp.moveaxis(array.reshape(*before, count, -1, *after), dim, 0)


def sum_at_owner(array, axis, dim):
    blocks = cut_along(array, dim, lax.axis_size(axis))
    arrived = lax.all_to_all(blocks, axis, split_axis=0, concat_axis=0, tiled=True)
    return arrived.sum(axis=0)


def rotate(vector, positions, turn_sign):
    half_dim = HD // 2
    frequency = THETA ** (-2.0 * jnp.arange(half_dim, dtype=jnp.float32) / HD)
    angles = positions.astype(jnp.float32)[:, None] * frequency[None, :]
    cosine = jnp.cos(angles)[:, None, :]
    sine_table = turn_sign * jnp.sin(angles)[:, None, :]
    shaped = vector.reshape(vector.shape[0], -1, HD)
    first_half = shaped[..., :half_dim]
    second_half = shaped[..., half_dim:]
    turned = jnp.concatenate(
        [
            first_half * cosine - second_half * sine_table,
            second_half * cosine + first_half * sine_table,
        ],
        -1,
    )
    return turned.reshape(vector.shape)


def body(activations, queries, out_grad, key_weight, value_weight, sessions):
    score_scale = 1.0 / math.sqrt(HD)
    tok_rows = activations.shape[0]
    ctx_count = lax.axis_size("ctx")
    total_rows = ctx_count * tok_rows
    key_block = min(total_rows, tok_rows * max(1, 512 // tok_rows))
    is_long = lax.axis_index("group") == 0
    own_first = lax.axis_index("ctx") * tok_rows
    local_rows = jnp.arange(tok_rows, dtype=jnp.int32)
    query_rows = own_first + local_rows
    positions = jnp.where(is_long, query_rows, local_rows)
    own_sessions = sessions[0]
    kv_cols = key_weight.shape[1]
    kv_heads = kv_cols // HD
    group_heads = HQ // KVH
    both_weights = jnp.concatenate([key_weight, value_weight], 1)
    whole_weights = lax.all_gather(both_weights, "ctx", axis=0, tiled=True)
    projected = jnp.dot(activations, whole_weights, preferred_element_type=jnp.float32)
    rotated_keys = rotate(projected[:, :kv_cols], positions, 1.0).astype(jnp.bfloat16)
    value_rows = projected[:, kv_cols:].astype(jnp.bfloat16)
    rotated = rotate(queries.astype(jnp.float32), positions, 1.0).astype(jnp.bfloat16)
    query_heads = rotated.reshape(tok_rows, kv_heads, group_heads, HD)
    grad_heads = out_grad.reshape(tok_rows, kv_heads, group_heads, HD)
    context = lax.all_gather(
        jnp.concatenate([rotated_keys, value_rows], 1), "ctx", axis=0, tiled=True
    )
    first_block = jnp.where(is_long, 0, own_first // key_block)
    stop_block = own_first // key_block + 1

    def block_scores(block_index):
        block_first = (block_index * key_block).astype(jnp.int32)
        block_kv = lax.dynamic_slice_in_dim(context, block_first, key_block, 0)
        block_keys = block_kv[:, :kv_cols].reshape(key_block, kv_heads, HD)
        block_values = block_kv[:, kv_cols:].reshape(key_block, kv_heads, HD)
        key_rows = block_first + jnp.arange(key_block, dtype=jnp.int32)
        key_sessions = lax.dynamic_update_slice(
            jnp.full((key_block,), -1, jnp.int32), own_sessions, (own_first - block_first,)
        )
        same_session = own_sessions[:, None] == key_sessions[None, :]
        allowed = (key_rows[None, :] <= query_rows[:, None]) & (is_long | same_session)
        scores = (
            jnp.einsum(
                "qkgd,skd->kgqs", query_heads, block_keys, preferred_element_type=jnp.float32
            )
            * score_scale
        )
        scores = jnp.where(allowed[None, None], scores, -jnp.inf)
        return (scores, block_keys, block_values, block_first)

    def max_pass(block_index, loop_state):
        running_max, running_sum = loop_state
        scores = block_scores(block_index)[0]
        new_max = jnp.maximum(running_max, jnp.max(scores, -1))
        running_sum = running_sum * jnp.exp(running_max - new_max) + jnp.sum(
            jnp.exp(scores - new_max[..., None]), -1
        )
        return (new_max, running_sum)

    stat_shape = (kv_heads, group_heads, tok_rows)
    row_max, row_total = lax.fori_loop(
        first_block,
        stop_block,
        max_pass,
        (jnp.full(stat_shape, -jnp.inf, jnp.float32), jnp.zeros(stat_shape, jnp.float32)),
    )
    log_total = row_max + jnp.log(row_total)

    def output_pass(block_index, running):
        scores, block_keys, block_values, block_first = block_scores(block_index)
        rounded_weights = jnp.exp(scores - log_total[..., None]).astype(jnp.bfloat16)
        return running + jnp.einsum(
            "kgqs,skd->qkgd", rounded_weights, block_values, preferred_element_type=jnp.float32
        )

    attended = lax.fori_loop(
        first_block,
        stop_block,
        output_pass,
        jnp.zeros((tok_rows, kv_heads, group_heads, HD), jnp.float32),
    )
    attention = attended.reshape(tok_rows, kv_heads * group_heads * HD).astype(jnp.bfloat16)
    out_dot = jnp.einsum(
        "qkgd,qkgd->kgq",
        grad_heads.astype(jnp.float32),
        attention.astype(jnp.float32).reshape(tok_rows, kv_heads, group_heads, HD),
    )

    def grad_pass(block_index, loop_state):
        query_acc, key_buffer = loop_state
        scores, block_keys, block_values, block_first = block_scores(block_index)
        weights = jnp.exp(scores - log_total[..., None])
        rounded_weights = weights.astype(jnp.bfloat16)
        prob_grad = jnp.einsum(
            "qkgd,skd->kgqs", grad_heads, block_values, preferred_element_type=jnp.float32
        )
        score_grad = (weights * (prob_grad - out_dot[..., None])).astype(jnp.bfloat16)
        query_acc = query_acc + jnp.einsum(
            "kgqs,skd->qkgd", score_grad, block_keys, preferred_element_type=jnp.float32
        )
        key_part = (
            jnp.einsum(
                "kgqs,qkgd->skd", score_grad, query_heads, preferred_element_type=jnp.float32
            )
            * score_scale
        )
        value_part = jnp.einsum(
            "kgqs,qkgd->skd", rounded_weights, grad_heads, preferred_element_type=jnp.float32
        )
        update = jnp.concatenate(
            [key_part.reshape(key_block, kv_cols), value_part.reshape(key_block, kv_cols)], 1
        )
        key_buffer = lax.dynamic_update_slice(key_buffer, update, (block_first, jnp.int32(0)))
        return (query_acc, key_buffer)

    query_acc, key_buffer = lax.fori_loop(
        first_block,
        stop_block,
        grad_pass,
        (
            jnp.zeros((tok_rows, kv_heads, group_heads, HD), jnp.float32),
            jnp.zeros((total_rows, 2 * kv_cols), jnp.float32),
        ),
    )
    query_grad = rotate(
        query_acc.reshape(tok_rows, kv_heads * group_heads * HD) * score_scale, positions, -1.0
    ).astype(jnp.bfloat16)
    summed = lax.psum_scatter(key_buffer, "ctx", scatter_dimension=0, tiled=True)
    key_grad = rotate(summed[:, :kv_cols], positions, -1.0).astype(jnp.bfloat16)
    value_grad = summed[:, kv_cols:].astype(jnp.bfloat16)
    kv_grads = jnp.concatenate([key_grad, value_grad], 1)
    input_terms = lax.dot_general(
        kv_grads, whole_weights, (((1,), (1,)), ((), ())), preferred_element_type=jnp.float32
    )
    input_grad = sum_at_owner(input_terms, "tp", 1).astype(jnp.bfloat16)
    column_rows = lax.all_to_all(
        activations, ("group", "ctx"), split_axis=1, concat_axis=0, tiled=True
    )
    owned_rows = lax.dot_general(
        column_rows,
        lax.all_gather(kv_grads, ("group", "ctx"), axis=0, tiled=True),
        (((0,), (0,)), ((), ())),
        preferred_element_type=jnp.float32,
    )
    key_weight_grad = owned_rows[:, :kv_cols]
    value_weight_grad = owned_rows[:, kv_cols:]
    return (attention, query_grad, key_weight_grad, value_weight_grad, input_grad)


def solution(mesh):
    placed = (
        P(("group", "ctx"), None),
        P(("group", "ctx"), "tp"),
        P(("group", "ctx"), "tp"),
        P("ctx", "tp"),
        P("ctx", "tp"),
        P("ctx", None),
    )
    return jax.shard_map(
        body,
        mesh=mesh,
        in_specs=placed,
        out_specs=(
            P(("group", "ctx"), "tp"),
            P(("group", "ctx"), "tp"),
            P(("group", "ctx"), "tp"),
            P(("group", "ctx"), "tp"),
            P(("group", "ctx"), "tp"),
        ),
        check_vma=False,
    )
```

profile of v0, /device:TPU:8, one launch (start us, length us, event | category | flops | bytes accessed | tf_op | source)
XLA Modules:
  0.0 707.3 jit_solution(11987555391099404159)
XLA Ops:
  7.2 1.5 pad_maximum_fusion.2
  8.9 116.2 %all-gather.4.cloned.1.call-done = bf16[8192,256]{1,0:T(8,128)(2,1)} async-done(((bf16[256,256]{1,0:T(8,128)(2,1)}), bf16[8192,256]{1,0:T(8,128)(2,1)}) %all-gather.4.cloned.1.call-update) | async-done | bytes 4194320 | tf_op jit(solution)/shard_map/all_gather | solution.py:59
  125.1 4.1 convolution_bitcast_fusion.5
  131.9 91.5 %all-gather.6.cloned.1.call-done = bf16[4096,256]{0,1:T(8,128)(2,1)} async-done(((bf16[128,256]{0,1:T(8,128)(2,1)}), bf16[4096,256]{0,1:T(8,128)(2,1)}) %all-gather.6.cloned.1.call-update) | async-done | bytes 2097168 | tf_op jit(solution)/shard_map/all_gather | solution.py:66
  223.4 3.3 copy.81
  226.7 1.5 while.40
  228.8 2.0 while.41
  229.3 1.5 fusion.85
  230.9 1.0 bitcast_convert_fusion
  231.8 1.4 copy.105
  233.5 2.5 broadcast_in_dim.52
  236.0 6.4 while.42
  236.5 1.5 fusion.93
  237.9 1.3 fusion.94
  239.3 1.3 fusion.95
  241.5 0.9 maximum_dynamic-update-slice_fusion.2
  242.4 1.6 copy-done
  244.0 2.5 copy.87
  246.5 70.4 %all-to-all-start = ((bf16[128,64,128]{0,2,1:T(8,128)(2,1)}), bf16[128,64,128]{0,2,1:T(8,128)(2,1)S(1)}, u32[]{:S(2)}, u32[]{:S(2)}) async-start(bf16[128,64,128]{0,2,1:T(8,128)(2,1)} %bitcast.241), calls=%async_computation.1 | async-start | bytes 4194304 | tf_op jit(solution)/shard_map/all_to_all | solution.py:177
  317.0 260.9 %reduce-scatter.2.cloned.1.call-done = f32[128,256]{0,1:T(8,128)} async-done(((f32[4096,256]{0,1:T(8,128)}), f32[128,256]{0,1:T(8,128)}) %reduce-scatter.2.cloned.1.call-update) | async-done | bytes 131088 | tf_op jit(solution)/shard_map/reduce_scatter | solution.py:169
  577.9 0.8 slice.125
  578.8 0.8 slice_bitcast_fusion
  580.5 3.7 fusion.60
  584.2 2.2 copy.114
  586.4 1.3 copy-done.1
  587.7 5.1 all-to-all-start.1
  592.9 3.3 copy.88
  596.2 0.8 copy.107
  597.2 0.8 copy.108
  598.0 94.4 %all-to-all-done.1 = f32[4,128,2048]{2,1,0:T(8,128)} async-done(((f32[4,128,2048]{2,1,0:T(8,128)}), f32[4,128,2048]{2,1,0:T(8,128)}, u32[]{:S(2)}, u32[]{:S(2)}) %all-to-all-start.1) | async-done | bytes 4194336 | tf_op jit(solution)/shard_map/all_to_all | solution.py:20
  692.4 3.4 reduce_sum.20
  695.9 3.4 convolution_bitcast_fusion.4
  (80 shorter events, 9.3 us)
Async XLA Ops:
  7.2 117.9 %all-gather.4.cloned.1.call-start = ((), (), s32[]{:S(2)}) async-start(), calls=%async_computation.3 | async-start | bytes 4325376 | tf_op jit(solution)/shard_map/all_gather | solution.py:59
  8.8 214.6 %all-gather.6.cloned.1.call-start = ((), (), s32[]{:S(2)}) async-start(), calls=%async_computation.4 | async-start | bytes 2162688 | tf_op jit(solution)/shard_map/all_gather | solution.py:66
  8.9 121.5 %copy-start.8 = (f32[128]{0:T(128)}, f32[128]{0:T(128)S(1)}, u32[]{:S(2)}) copy-start(f32[128]{0:T(128)S(1)} %fusion.59) | copy-start | bytes 1540
  8.9 121.4 %copy-start.6 = (bf16[128,1024]{1,0:T(8,128)(2,1)S(1)}, bf16[128,1024]{1,0:T(8,128)(2,1)}, u32[]{:S(2)}) copy-start(bf16[128,1024]{1,0:T(8,128)(2,1)} %param.13) | copy-start | bytes 786436
  129.3 1.6 copy-start.4
  130.2 447.8 %reduce-scatter.2.cloned.1.call-start = ((), (), s32[]{:S(2)}) async-start(), calls=%async_computation.5 | async-start | bytes 4325376 | tf_op jit(solution)/shard_map/reduce_scatter | solution.py:169
  131.9 94.8 %copy-start.7 = (s32[1,128]{1,0:T(1,128)S(1)}, s32[1,128]{1,0:T(1,128)}, u32[]{:S(2)}) copy-start(s32[1,128]{1,0:T(1,128)} %param.17) | copy-start | bytes 1540
  230.9 2.6 copy-start.2
  230.9 2.3 copy-start.5
  242.4 1.6 copy-start
  246.5 333.1 %copy-start.9 = (f32[128]{0:T(128)S(1)}, f32[128]{0:T(128)}, u32[]{:S(2)}) copy-start(f32[128]{0:T(128)} %copy-done.8) | copy-start | bytes 1540
  246.5 339.9 %all-to-all-start = ((bf16[128,64,128]{0,2,1:T(8,128)(2,1)}), bf16[128,64,128]{0,2,1:T(8,128)(2,1)S(1)}, u32[]{:S(2)}, u32[]{:S(2)}) async-start(bf16[128,64,128]{0,2,1:T(8,128)(2,1)} %bitcast.241), calls=%async_computation.1 | async-start | bytes 4194304 | tf_op jit(solution)/shard_map/all_to_all | solution.py:177
  317.0 378.9 %all-gather.8.cloned.1.call-start = ((), (), s32[]{:S(2)}) async-start(), calls=%async_computation.6 | async-start | bytes 4259840 | tf_op jit(solution)/shard_map/all_gather | solution.py:182
  586.4 1.3 copy-start.1
  587.7 104.7 %all-to-all-start.1 = ((f32[4,128,2048]{2,1,0:T(8,128)}), f32[4,128,2048]{2,1,0:T(8,128)}, u32[]{:S(2)}, u32[]{:S(2)}) async-start(f32[4,128,2048]{2,1,0:T(8,128)} %bitcast.237), calls=%async_computation.2 | async-start | bytes 8388608 | tf_op jit(solution)/shard_map/all_to_all | solution.py:20
  592.9 3.3 copy-start.3
Sparse Core Ops, SparseCore 0:
  12.1 113.0 all-gather.3
  130.3 93.0 all-gather.5
  242.6 335.3 reduce-scatter.1
  581.7 100.2 all-gather.7
where the time goes:
time: 709 us; the launch traced here: 707 us
  waiting for transfers between devices  563 us (79%)
  starting transfers between devices  75.7 us (11%)
  local copies, waits for them, and re-layouts  25 us (4%)
  matrix products  18.2 us (3%)
  between operations  14.1 us (2%)
  other arithmetic  10.9 us (2%)
    reduce_scatter x1, waiting for transfers between devices, body(): lax.psum_scatter(key_buffer, 'ctx', scatter_dimension=0, tiled=True)  261 us
    all_gather x1, waiting for transfers between devices, body(): whole_weights = lax.all_gather(both_weights, 'ctx', axis=0, tiled=True)  116 us
    all_to_all x1, waiting for transfers between devices, sum_at_owner(): lax.all_to_all(blocks, axis, split_axis=0, concat_axis=0, tiled=True)  94.4 us
    all_gather x1, waiting for transfers between devices, body(): lax.all_gather(jnp.concatenate([rotated_keys, value_rows], 1), 'ctx', axi...  91.5 us
    all_to_all x1, starting transfers between devices, body(): lax.all_to_all(activations, ('group', 'ctx'), split_axis=1, concat_axis=0...  70.4 us
  transfers between devices with their start and end apart: 6, of which 4 were waited for; matrix products, arithmetic and copies ran while one was open for 3% of the time, Pallas kernels for 0%

commit v1 on v0

--- a/solution.py
+++ b/solution.py
@@ -8,6 +8,13 @@
 KVH = 4
 HD = 128
 THETA = 500000.0
+
+
+def try_all_spans(sheet):
+    opened = lax.axis_size("ctx")
+    response = jnp.stack(opened * [sheet], axis=0)
+    parts_out = lax.all_to_all(response, "ctx", 0, 0)
+    return jnp.concatenate(parts_out, 0)
 
 
 def cut_along(array, dim, count):
@@ -63,9 +70,7 @@
     rotated = rotate(queries.astype(jnp.float32), positions, 1.0).astype(jnp.bfloat16)
     query_heads = rotated.reshape(tok_rows, kv_heads, group_heads, HD)
     grad_heads = out_grad.reshape(tok_rows, kv_heads, group_heads, HD)
-    context = lax.all_gather(
-        jnp.concatenate([rotated_keys, value_rows], 1), "ctx", axis=0, tiled=True
-    )
+    context = try_all_spans(jnp.concatenate([rotated_keys, value_rows], 1))
     first_block = jnp.where(is_long, 0, own_first // key_block)
     stop_block = own_first // key_block + 1
 

time: 709 us -> 668 us (0.942)
  waiting for transfers between devices: 563 us -> 494 us
  starting transfers between devices: 75.7 us -> 105 us
    all_gather x1 -> x0, waiting for transfers between devices: 91.5 us -> none  [body(): lax.all_gather(jnp.concatenate([rotated_keys, value_rows], 1), 'ctx', axi...]
    all_to_all x0 -> x1, waiting for transfers between devices: none -> 24.5 us  [try_all_spans(): parts_out = lax.all_to_all(response, 'ctx', 0, 0)]
    all_to_all x1, starting transfers between devices: 5.11 us -> 23.4 us  [sum_at_owner(): lax.all_to_all(blocks, axis, split_axis=0, concat_axis=0, tiled=True)]
where the time goes in v1:
time: 668 us; the launch traced here: 665 us
  waiting for transfers between devices  494 us (74%)
  starting transfers between devices  105 us (16%)
  local copies, waits for them, and re-layouts  23.6 us (4%)
  matrix products  18.3 us (3%)
  between operations  14.1 us (2%)
  other arithmetic  10.2 us (2%)
    reduce_scatter x1, waiting for transfers between devices, body(): lax.psum_scatter(key_buffer, 'ctx', scatter_dimension=0, tiled=True)  262 us
    all_gather x1, waiting for transfers between devices, body(): whole_weights = lax.all_gather(both_weights, 'ctx', axis=0, tiled=True)  116 us
    all_to_all x1, waiting for transfers between devices, sum_at_owner(): lax.all_to_all(blocks, axis, split_axis=0, concat_axis=0, tiled=True)  91.8 us
    all_to_all x1, starting transfers between devices, body(): lax.all_to_all(activations, ('group', 'ctx'), split_axis=1, concat_axis=0...  74.8 us
    all_to_all x1, waiting for transfers between devices, try_all_spans(): parts_out = lax.all_to_all(response, 'ctx', 0, 0)  24.5 us
    all_to_all x1, starting transfers between devices, sum_at_owner(): lax.all_to_all(blocks, axis, split_axis=0, concat_axis=0, tiled=True)  23.4 us
  transfers between devices with their start and end apart: 6, of which 4 were waited for; matrix products, arithmetic and copies ran while one was open for 3% of the time, Pallas kernels for 0%

profile of v1, /device:TPU:8, one launch (start us, length us, event | category | flops | bytes accessed | tf_op | source)
XLA Modules:
  0.0 665.4 jit_solution(16815579231978557974)
XLA Ops:
  7.2 1.5 pad_maximum_fusion.2
  8.8 116.3 %all-gather.3.cloned.1.call-done = bf16[8192,256]{1,0:T(8,128)(2,1)} async-done(((bf16[256,256]{1,0:T(8,128)(2,1)}), bf16[8192,256]{1,0:T(8,128)(2,1)}) %all-gather.3.cloned.1.call-update) | async-done | bytes 4194320 | tf_op jit(solution)/shard_map/all_gather | solution.py:66
  125.1 4.1 convolution_bitcast_fusion.5
  129.6 1.6 stack.2
  131.2 6.3 all-to-all-start
  139.4 24.5 %all-to-all-done = bf16[32,128,256]{2,1,0:T(8,128)(2,1)S(1)} async-done(((bf16[32,128,256]{2,1,0:T(8,128)(2,1)}), bf16[32,128,256]{2,1,0:T(8,128)(2,1)S(1)}, u32[]{:S(2)}, u32[]{:S(2)}) %all-to-all-start) | async-done | bytes 2097184 | tf_op jit(solution)/shard_map/all_to_all | solution.py:16
  163.9 1.4 while.40
  166.0 2.0 while.41
  166.6 1.5 fusion.85
  168.1 1.0 bitcast_convert_fusion
  169.1 1.4 copy.97
  170.8 2.5 broadcast_in_dim.52
  173.2 6.3 while.42
  173.7 1.5 fusion.93
  175.2 1.3 fusion.94
  176.5 1.3 fusion.95
  178.7 0.9 maximum_dynamic-update-slice_fusion.2
  179.6 1.6 copy-done
  181.2 2.5 copy.79
  183.7 74.8 %all-to-all-start.1 = ((bf16[128,64,128]{0,2,1:T(8,128)(2,1)}), bf16[128,64,128]{0,2,1:T(8,128)(2,1)S(1)}, u32[]{:S(2)}, u32[]{:S(2)}) async-start(bf16[128,64,128]{0,2,1:T(8,128)(2,1)} %bitcast.242), calls=%async_computation.2 | async-start | bytes 4194304 | tf_op jit(solution)/shard_map/all_to_all | solution.py:182
  258.6 261.6 %reduce-scatter.2.cloned.1.call-done = f32[128,256]{0,1:T(8,128)} async-done(((f32[4096,256]{0,1:T(8,128)}), f32[128,256]{0,1:T(8,128)}) %reduce-scatter.2.cloned.1.call-update) | async-done | bytes 131088 | tf_op jit(solution)/shard_map/reduce_scatter | solution.py:174
  520.2 0.8 slice.125
  522.8 3.7 fusion.60
  526.4 2.2 copy.106
  528.7 1.3 copy-done.1
  530.0 23.4 %all-to-all-start.2 = ((f32[4,128,2048]{2,1,0:T(8,128)}), f32[4,128,2048]{2,1,0:T(8,128)}, u32[]{:S(2)}, u32[]{:S(2)}) async-start(f32[4,128,2048]{2,1,0:T(8,128)} %bitcast.238), calls=%async_computation.3 | async-start | bytes 8388608 | tf_op jit(solution)/shard_map/all_to_all | solution.py:27
  553.4 3.3 copy.80
  556.7 0.9 copy.99
  557.7 0.9 copy.100
  558.6 91.8 %all-to-all-done.2 = f32[4,128,2048]{2,1,0:T(8,128)} async-done(((f32[4,128,2048]{2,1,0:T(8,128)}), f32[4,128,2048]{2,1,0:T(8,128)}, u32[]{:S(2)}, u32[]{:S(2)}) %all-to-all-start.2) | async-done | bytes 4194336 | tf_op jit(solution)/shard_map/all_to_all | solution.py:27
  650.4 3.4 reduce_sum.20
  653.9 3.5 convolution_bitcast_fusion.4
  (80 shorter events, 9.7 us)
Async XLA Ops:
  7.2 117.9 %all-gather.3.cloned.1.call-start = ((), (), s32[]{:S(2)}) async-start(), calls=%async_computation.4 | async-start | bytes 4325376 | tf_op jit(solution)/shard_map/all_gather | solution.py:66
  8.8 129.0 %copy-start.8 = (f32[128]{0:T(128)}, f32[128]{0:T(128)S(1)}, u32[]{:S(2)}) copy-start(f32[128]{0:T(128)S(1)} %fusion.59) | copy-start | bytes 1540
  131.2 6.4 copy-start.6
  131.2 32.7 %all-to-all-start = ((bf16[32,128,256]{2,1,0:T(8,128)(2,1)}), bf16[32,128,256]{2,1,0:T(8,128)(2,1)S(1)}, u32[]{:S(2)}, u32[]{:S(2)}) async-start(bf16[32,128,256]{2,1,0:T(8,128)(2,1)} %stack.2), calls=%async_computation | async-start | bytes 4194304 | tf_op jit(solution)/shard_map/all_to_all | solution.py:16
  137.6 1.0 copy-start.4
  137.6 26.4 %copy-start.7 = (s32[1,128]{1,0:T(1,128)S(1)}, s32[1,128]{1,0:T(1,128)}, u32[]{:S(2)}) copy-start(s32[1,128]{1,0:T(1,128)} %param.17) | copy-start | bytes 1540
  137.6 382.6 %reduce-scatter.2.cloned.1.call-start = ((), (), s32[]{:S(2)}) async-start(), calls=%async_computation.5 | async-start | bytes 4325376 | tf_op jit(solution)/shard_map/reduce_scatter | solution.py:174
  168.1 2.6 copy-start.2
  168.1 2.3 copy-start.5
  179.6 1.6 copy-start
  183.7 338.2 %copy-start.9 = (f32[128]{0:T(128)S(1)}, f32[128]{0:T(128)}, u32[]{:S(2)}) copy-start(f32[128]{0:T(128)} %copy-done.8) | copy-start | bytes 1540
  183.7 345.0 %all-to-all-start.1 = ((bf16[128,64,128]{0,2,1:T(8,128)(2,1)}), bf16[128,64,128]{0,2,1:T(8,128)(2,1)S(1)}, u32[]{:S(2)}, u32[]{:S(2)}) async-start(bf16[128,64,128]{0,2,1:T(8,128)(2,1)} %bitcast.242), calls=%async_computation.2 | async-start | bytes 4194304 | tf_op jit(solution)/shard_map/all_to_all | solution.py:182
  258.5 395.4 %all-gather.5.cloned.1.call-start = ((), (), s32[]{:S(2)}) async-start(), calls=%async_computation.6 | async-start | bytes 4259840 | tf_op jit(solution)/shard_map/all_gather | solution.py:187
  528.7 1.3 copy-start.1
  530.0 120.4 %all-to-all-start.2 = ((f32[4,128,2048]{2,1,0:T(8,128)}), f32[4,128,2048]{2,1,0:T(8,128)}, u32[]{:S(2)}, u32[]{:S(2)}) async-start(f32[4,128,2048]{2,1,0:T(8,128)} %bitcast.238), calls=%async_computation.3 | async-start | bytes 8388608 | tf_op jit(solution)/shard_map/all_to_all | solution.py:27
  553.4 3.3 copy-start.3
Sparse Core Ops, SparseCore 0:
  12.1 113.0 all-gather.2
  179.7 340.4 reduce-scatter.1
  524.1 114.6 all-gather.4
